TPU v7x, 32 devices: a whole 2x2x4 slice. The times are simulated.
32 devices in a mesh: dp: 8 (over z, y), tensor: 4 (over x, core).
Axes of the slice: x: 2, y: 2, z: 4, core: 2. Of those that a mesh axis runs over, the one named last changes fastest.
Arguments:
- tokens: bfloat16 [8192, 768], P('dp'), may hold values from -6 to 6
- segment_ids: int32 [16, 512], P('dp'), may hold values from 0 to 3, never falling along the last dimension, each value on 1 to 256 neighbouring positions
- qkv_weight: bfloat16 [768, 3, 12, 64], P(None, None, 'tensor'), may hold values from -0.21875 to 0.21875
- qkv_bias: bfloat16 [2, 12, 64], P(None, 'tensor'), may hold values from -3 to 3
- output_weight: bfloat16 [12, 64, 768], P('tensor'), may hold values from -1.25 to 1.25
- output_bias: bfloat16 [768], replicated, may hold values from -2 to 2
- first_gain: bfloat16 [768], replicated, may hold values from 0.5 to 1.5
- first_shift: bfloat16 [768], replicated, may hold values from -2 to 2
- up_weight: bfloat16 [768, 3072], P(None, 'tensor'), may hold values from -0.21875 to 0.21875
- up_bias: bfloat16 [48, 64], P('tensor'), may hold values from -3 to 3
- down_weight: bfloat16 [3072, 768], P('tensor'), may hold values from -0.109375 to 0.109375
- down_bias: bfloat16 [768], replicated, may hold values from -2 to 2
- second_gain: bfloat16 [768], replicated, may hold values from 0.5 to 1.5
- second_shift: bfloat16 [768], replicated, may hold values from -2 to 2
- cotangent: bfloat16 [8192, 768], P('dp'), may hold values from -6 to 6
Outputs:
- layer_out: bfloat16 [8192, 768], P(('dp', 'tensor'))
- tokens_grad: bfloat16 [8192, 768], P(('dp', 'tensor'))
- qkv_weight_grad: float32 [768, 3, 12, 64], P('dp', None, 'tensor')
- qkv_bias_grad: float32 [2, 12, 64], P(None, 'tensor', 'dp')
- output_weight_grad: float32 [12, 64, 768], P('tensor', None, 'dp')
- output_bias_grad: float32 [768], P('dp')
- first_gain_grad: float32 [768], P('dp')
- first_shift_grad: float32 [768], P('dp')
- up_weight_grad: float32 [768, 3072], P('dp', 'tensor')
- up_bias_grad: float32 [48, 64], P('tensor', 'dp')
- down_weight_grad: float32 [3072, 768], P('tensor', 'dp')
- down_bias_grad: float32 [768], P('dp')
- second_gain_grad: float32 [768], P('dp')
- second_shift_grad: float32 [768], P('dp')
Inputs may be any that keep to these rules, and one draw needn't show every extreme that they name: `segment_ids`: along each row of 512 tokens the ids never fall; each id covers 1 to 256 tokens of its row.
All inputs are finite; a program needn't handle non-finite values.
Results may differ from a plain program's by a relative error of at most 0.02.
The roundings to bfloat16 on the way count: a program that leaves them out, or rounds other values in their place, can miss the bound.
Values may be sent and summed in bfloat16 or wider, within the bound.
A program may use at most 128 MiB of HBM per device.

v0:
```python
import jax
import jax.numpy as jnp
from jax import lax
from jax.sharding import PartitionSpec as P

HEAD = 64
SEQ = 512
EPS = 1e-12


def normalize(rows_in, gain_vec, shift_vec):
    center = rows_in - jnp.mean(rows_in, axis=-1, keepdims=True)
    spread = jnp.mean(center * center, axis=-1, keepdims=True)
    return center * lax.rsqrt(spread + EPS) * gain_vec + shift_vec


def norm_back(rows_in, gain_vec, shift_vec, grad_out):
    unused, pull_back = jax.vjp(normalize, rows_in, gain_vec, shift_vec)
    return pull_back(grad_out)


def gelu_exact(values_in):
    return jax.nn.gelu(values_in, approximate=False)


def head_scores(queries, keys_low, same_doc):
    scores = jnp.einsum(
        "rqhd,rkhd->rhqk", queries, keys_low, preferred_element_type=jnp.float32
    ) * HEAD ** (-0.5)
    return jnp.where(same_doc[:, None], scores, -1e30)


def attend(queries, keys_low, values_low, same_doc):
    scores = head_scores(queries, keys_low, same_doc)
    row_top = jnp.max(scores, axis=-1, keepdims=True)
    expo_vals = jnp.exp(scores - row_top)
    row_total = jnp.sum(expo_vals, axis=-1, keepdims=True)
    attn_probs = (expo_vals / row_total).astype(jnp.bfloat16)
    context = jnp.einsum(
        "rhqk,rkhd->rqhd", attn_probs, values_low, preferred_element_type=jnp.float32
    )
    return (context.astype(jnp.bfloat16), row_top + jnp.log(row_total))


def attend_back(queries, keys_low, values_low, same_doc, log_total, d_context):
    probs_full = jnp.exp(head_scores(queries, keys_low, same_doc) - log_total)
    d_probs = jnp.einsum(
        "rqhd,rkhd->rhqk", d_context, values_low, preferred_element_type=jnp.float32
    )
    inner_sum = jnp.sum(probs_full * d_probs, axis=-1, keepdims=True)
    d_scores = (probs_full * (d_probs - inner_sum)).astype(jnp.bfloat16)
    factor = HEAD ** (-0.5)
    d_query = (
        jnp.einsum("rhqk,rkhd->rqhd", d_scores, keys_low, preferred_element_type=jnp.float32)
        * factor
    )
    d_keys = (
        jnp.einsum("rhqk,rqhd->rkhd", d_scores, queries, preferred_element_type=jnp.float32)
        * factor
    )
    d_values = jnp.einsum(
        "rhqk,rqhd->rkhd",
        probs_full.astype(jnp.bfloat16),
        d_context,
        preferred_element_type=jnp.float32,
    )
    return (d_query, d_keys, d_values)


def body(
    tokens,
    segment_ids,
    qkv_weight,
    qkv_bias,
    output_weight,
    output_bias,
    first_gain,
    first_shift,
    up_weight,
    up_bias,
    down_weight,
    down_bias,
    second_gain,
    second_shift,
    cotangent,
):
    token_count = tokens.shape[0]
    row_count = token_count // SEQ
    head_count = qkv_weight.shape[2]
    head_width = head_count * HEAD
    share_rows = token_count // lax.axis_size("tensor")
    offset = lax.axis_index("tensor") * share_rows
    same_doc = segment_ids[:, :, None] == segment_ids[:, None, :]
    qkv_matrix = qkv_weight.reshape(qkv_weight.shape[0], 3 * head_width)
    out_matrix = output_weight.reshape(head_width, output_weight.shape[2])
    bias_rows = qkv_bias.astype(jnp.float32).reshape(2, head_width)
    gain_first = first_gain.astype(jnp.float32)
    shift_first = first_shift.astype(jnp.float32)
    gain_second = second_gain.astype(jnp.float32)
    shift_second = second_shift.astype(jnp.float32)

    def split_heads(matrix):
        return matrix.reshape(row_count, SEQ, head_count, HEAD)

    mixed_proj = jnp.dot(tokens, qkv_matrix, preferred_element_type=jnp.float32).reshape(
        token_count, 3, head_width
    )
    queries = (mixed_proj[:, 0] + bias_rows[0]).astype(jnp.bfloat16)
    keys_low = mixed_proj[:, 1].astype(jnp.bfloat16)
    values_low = (mixed_proj[:, 2] + bias_rows[1]).astype(jnp.bfloat16)
    context, log_total = attend(
        split_heads(queries), split_heads(keys_low), split_heads(values_low), same_doc
    )
    context = context.reshape(token_count, head_width)
    attn_terms = jnp.dot(context, out_matrix, preferred_element_type=jnp.float32)
    attn_total = lax.psum(attn_terms.astype(jnp.bfloat16), "tensor").astype(jnp.float32)
    residual = tokens.astype(jnp.float32)
    grad_rows = cotangent.astype(jnp.float32)
    first_in = residual + attn_total + output_bias.astype(jnp.float32)
    first_out = normalize(first_in, gain_first, shift_first)
    first_low = first_out.astype(jnp.bfloat16)
    hidden = jnp.dot(first_low, up_weight, preferred_element_type=jnp.float32) + up_bias.astype(
        jnp.float32
    ).reshape(-1)
    active, gelu_pull = jax.vjp(gelu_exact, hidden)
    active_low = active.astype(jnp.bfloat16)
    down_terms = jnp.dot(active_low, down_weight, preferred_element_type=jnp.float32)
    down_total = lax.psum(down_terms.astype(jnp.bfloat16), "tensor").astype(jnp.float32)
    second_in = first_out + down_total + down_bias.astype(jnp.float32)
    layer_full = normalize(second_in, gain_second, shift_second).astype(jnp.bfloat16)
    d_second, gain_second_grad, shift_second_grad = norm_back(
        second_in, gain_second, shift_second, grad_rows
    )
    down_bias_grad = jnp.sum(d_second, axis=0)
    d_second_low = d_second.astype(jnp.bfloat16)
    down_grad = jnp.einsum(
        "tf,td->fd", active_low, d_second_low, preferred_element_type=jnp.float32
    )
    d_active = jnp.einsum(
        "td,fd->tf", d_second_low, down_weight, preferred_element_type=jnp.float32
    )
    (d_hidden,) = gelu_pull(d_active)
    up_bias_grad = jnp.sum(d_hidden, axis=0).reshape(up_bias.shape)
    d_hidden_low = d_hidden.astype(jnp.bfloat16)
    up_grad = jnp.einsum("td,tf->df", first_low, d_hidden_low, preferred_element_type=jnp.float32)
    up_terms = jnp.einsum("tf,df->td", d_hidden_low, up_weight, preferred_element_type=jnp.float32)
    up_total = lax.psum(up_terms.astype(jnp.bfloat16), "tensor").astype(jnp.float32)
    d_first = d_second + up_total
    d_first_in, gain_first_grad, shift_first_grad = norm_back(
        first_in, gain_first, shift_first, d_first
    )
    out_bias_grad = jnp.sum(d_first_in, axis=0)
    d_attn_low = d_first_in.astype(jnp.bfloat16)
    out_grad = jnp.einsum("tc,td->cd", context, d_attn_low, preferred_element_type=jnp.float32)
    d_context = jnp.einsum(
        "td,cd->tc", d_attn_low, out_matrix, preferred_element_type=jnp.float32
    ).astype(jnp.bfloat16)
    d_query, d_keys, d_values = attend_back(
        split_heads(queries),
        split_heads(keys_low),
        split_heads(values_low),
        same_doc,
        log_total,
        split_heads(d_context),
    )
    d_query = d_query.reshape(token_count, head_width)
    d_keys = d_keys.reshape(token_count, head_width)
    d_values = d_values.reshape(token_count, head_width)
    qkv_bias_grad = jnp.stack([jnp.sum(d_query, axis=0), jnp.sum(d_values, axis=0)]).reshape(
        qkv_bias.shape
    )
    d_mixed = (
        jnp.stack([d_query, d_keys, d_values], axis=1)
        .astype(jnp.bfloat16)
        .reshape(token_count, 3 * head_width)
    )
    qkv_grad = jnp.einsum("td,tc->dc", tokens, d_mixed, preferred_element_type=jnp.float32).reshape(
        qkv_weight.shape
    )
    token_terms = jnp.einsum("tc,dc->td", d_mixed, qkv_matrix, preferred_element_type=jnp.float32)
    token_total = lax.psum(token_terms.astype(jnp.bfloat16), "tensor").astype(jnp.float32)
    tokens_grad = lax.dynamic_slice_in_dim(d_first_in + token_total, offset, share_rows, 0).astype(
        jnp.bfloat16
    )
    layer_out = lax.dynamic_slice_in_dim(layer_full, offset, share_rows, 0)
    small_grads = (
        out_bias_grad,
        gain_first_grad,
        shift_first_grad,
        down_bias_grad,
        gain_second_grad,
        shift_second_grad,
    )
    attn_parts = (
        lax.psum_scatter(qkv_grad, "dp", scatter_dimension=0, tiled=True),
        lax.psum_scatter(qkv_bias_grad, "dp", scatter_dimension=2, tiled=True),
        lax.psum_scatter(
            out_grad.reshape(output_weight.shape), "dp", scatter_dimension=2, tiled=True
        ),
        lax.psum_scatter(small_grads[0], "dp", scatter_dimension=0, tiled=True),
        lax.psum_scatter(small_grads[1], "dp", scatter_dimension=0, tiled=True),
        lax.psum_scatter(small_grads[2], "dp", scatter_dimension=0, tiled=True),
    )
    ffn_parts = (
        lax.psum_scatter(up_grad, "dp", scatter_dimension=0, tiled=True),
        lax.psum_scatter(up_bias_grad, "dp", scatter_dimension=1, tiled=True),
        lax.psum_scatter(down_grad, "dp", scatter_dimension=1, tiled=True),
        lax.psum_scatter(small_grads[3], "dp", scatter_dimension=0, tiled=True),
        lax.psum_scatter(small_grads[4], "dp", scatter_dimension=0, tiled=True),
        lax.psum_scatter(small_grads[5], "dp", scatter_dimension=0, tiled=True),
    )
    return (
        layer_out,
        tokens_grad,
        attn_parts[0],
        attn_parts[1],
        attn_parts[2],
        attn_parts[3],
        attn_parts[4],
        attn_parts[5],
        ffn_parts[0],
        ffn_parts[1],
        ffn_parts[2],
        ffn_parts[3],
        ffn_parts[4],
        ffn_parts[5],
    )


def solution(mesh):
    placed = (
        P("dp", None),
        P("dp", None),
        P(None, None, "tensor", None),
        P(None, "tensor", None),
        P("tensor", None, None),
        P(),
        P(),
        P(),
        P(None, "tensor"),
        P("tensor", None),
        P("tensor", None),
        P(),
        P(),
        P(),
        P("dp", None),
    )
    return jax.shard_map(
        body,
        mesh=mesh,
        in_specs=placed,
        out_specs=(
            P(("dp", "tensor"), None),
            P(("dp", "tensor"), None),
            P("dp", None, "tensor", None),
            P(None, "tensor", "dp"),
            P("tensor", None, "dp"),
            P("dp"),
            P("dp"),
            P("dp"),
            P("dp", "tensor"),
            P("tensor", "dp"),
            P("tensor", "dp"),
            P("dp"),
            P("dp"),
            P("dp"),
        ),
        check_vma=False,
    )
```

profile of v0, /device:TPU:0, one launch (start us, length us, event | category | flops | bytes accessed | tf_op | source)
XLA Modules:
  0.0 553.5 jit_solution(17935516750213851059)
XLA Ops:
  7.2 2.8 fusion.21
  10.2 1.0 fusion.64
  11.2 1.2 broadcast_compare_fusion
  12.7 0.7 squeeze.7
  13.4 2.1 squeeze.8
  15.5 2.5 fusion.66
  18.1 0.9 fusion
  19.0 1.6 copy-done.2
  20.7 1.3 fusion.29
  22.6 0.8 copy-done.11
  23.3 1.9 convolution_convert_fusion.3
  25.8 1.3 convert_element_type.130
  27.1 0.7 reshape.183
  27.7 43.2 %all-reduce.14.cloned.1.call-done = bf16[1024,768]{1,0:T(8,128)(2,1)} async-done(((bf16[1024,768]{1,0:T(8,128)(2,1)}), bf16[1024,768]{1,0:T(8,128)(2,1)}) %all-reduce.14.cloned.1.call-update) | async-done | bytes 1572880 | tf_op jit(solution)/shard_map/psum | solution.py:116
  70.9 2.1 fusion.17
  73.1 0.9 multiply_reduce_fusion.4
  73.9 0.6 copy-done.38
  74.6 9.9 %multiply_convert_fusion.1 = (bf16[1024,768]{1,0:T(8,128)(2,1)S(1)}, f32[1024,768]{1,0:T(8,128)}, f32[1024,768]{1,0:T(8,128)}) fusion(f32[768]{0:T(1024)S(1)} %copy-done.57, bf16[768,768]{1,0:T(8,128)(2,1)S(1)} %copy-done, f32[768]{0:T(1024)S(1)} %copy-done.47, f32[768]{0:T(1024)S(1)} %convert_element_type.129, f32[1024]{0:T(1024)S(1)} %fusion.49, ...), kind=kOutput, calls=%fused_computation.27 | convolution fusion | flops 1266941952 | bytes 12210176 | tf_op jit(solution)/shard_map/dot_general | solution.py:122
  84.5 1.2 copy-done.65
  85.7 2.5 convolution_convert_fusion.2
  88.3 1.3 convert_element_type.136
  89.6 1.3 convert_element_type.135
  90.8 40.5 %all-reduce.16.cloned.1.call-done = bf16[1024,768]{1,0:T(8,128)(2,1)} async-done(((bf16[1024,768]{1,0:T(8,128)(2,1)}), bf16[1024,768]{1,0:T(8,128)(2,1)}) %all-reduce.16.cloned.1.call-update) | async-done | bytes 1572880 | tf_op jit(solution)/shard_map/psum | solution.py:128
  131.4 3.3 fusion.62
  134.7 1.8 fusion.4
  136.5 3.6 fusion.61
  140.1 0.7 copy-done.67
  140.8 3.2 fusion.69
  144.0 1.2 copy-done.68
  145.2 2.6 convolution_convert_fusion.1
  147.9 0.7 log_add_fusion
  148.7 42.2 %all-reduce.18.cloned.1.call-done = bf16[1024,768]{1,0:T(8,128)(2,1)} async-done(((bf16[1024,768]{1,0:T(8,128)(2,1)}), bf16[1024,768]{1,0:T(8,128)(2,1)}) %all-reduce.18.cloned.1.call-update) | async-done | bytes 1572880 | tf_op jit(solution)/shard_map/psum | solution.py:147
  190.9 4.5 fusion.59
  195.4 2.6 multiply_reduce_fusion.1
  198.1 2.1 fusion.60
  200.2 1.8 copy-done.6
  201.9 0.7 convolution_convert_fusion.4
  202.9 5.4 fusion.67
  208.3 4.5 multiply_reduce_fusion
  212.9 1.8 multiply_convert_fusion
  214.7 1.1 fusion.26
  215.8 0.7 fusion.68
  218.7 1.0 copy-done.16
  219.8 3.8 convolution_convert_fusion
  223.6 2.4 fusion.19
  226.0 1.5 copy.79
  227.5 2.8 reshape.190
  230.4 2.3 convolution_bitcast_fusion
  232.7 3.0 copy.83
  235.9 5.4 fusion.51
  241.4 5.2 fusion.37
  246.8 0.6 dynamic-slice
  248.8 2.0 fusion.32
  250.8 37.6 %all-reduce.8 = (f32[2,3,64]{2,1,0:T(4,128)S(1)}, f32[768]{0:T(1024)S(1)}, f32[768]{0:T(1024)S(1)}, f32[768]{0:T(1024)S(1)}, f32[12,64]{1,0:T(8,128)S(1)}, /*ind...) all-reduce(f32[2,3,64]{2,1,0:T(4,128)S(1)} %pad_maximum_fusion, ...), channel_id=3, replica_groups=mesh['dp'=8,'tensor'=4] {'dp'}, use_global_device_ids=true, to_apply=%region_18.19.clone | all-reduce | flops 5760 | bytes 46080
  288.4 0.6 copy.69
  289.1 0.7 copy.70
  293.2 2.1 fusion.30
  295.3 37.1 %reduce-scatter.17.cloned.1.call-done = f32[96,192]{1,0:T(8,128)} async-done(((f32[768,192]{1,0:T(8,128)}), f32[96,192]{1,0:T(8,128)}) %reduce-scatter.17.cloned.1.call-update) | async-done | bytes 73744
  332.4 1.0 reshape.191
  333.4 0.8 copy.80
  334.2 67.8 %reduce-scatter.15.cloned.1.call-done = f32[96,576]{1,0:T(8,128)} async-done(((f32[768,576]{1,0:T(8,128)}), f32[96,576]{1,0:T(8,128)}) %reduce-scatter.15.cloned.1.call-update) | async-done | bytes 221200
  401.9 1.8 copy.84
  403.8 70.4 %reduce-scatter.13.cloned.1.call-done = f32[768,96]{0,1:T(8,128)} async-done(((f32[768,768]{0,1:T(8,128)}), f32[768,96]{0,1:T(8,128)}) %reduce-scatter.13.cloned.1.call-update) | async-done | bytes 294928 | tf_op jit(solution)/shard_map/reduce_scatter | solution.py:207
  474.1 72.3 %reduce-scatter.11.cloned.1.call-done = f32[96,768]{1,0:T(8,128)} async-done(((f32[768,768]{1,0:T(8,128)}), f32[96,768]{1,0:T(8,128)}) %reduce-scatter.11.cloned.1.call-update) | async-done | bytes 294928 | tf_op jit(solution)/shard_map/reduce_scatter | solution.py:205
  (186 shorter events, 8.3 us)
Async XLA Ops:
  7.2 67.4 %copy-start = (bf16[768,768]{1,0:T(8,128)(2,1)S(1)}, bf16[768,768]{1,0:T(8,128)(2,1)}, u32[]{:S(2)}) copy-start(bf16[768,768]{1,0:T(8,128)(2,1)} %param.23) | copy-start | bytes 3538948
  7.2 63.7 %all-reduce.14.cloned.1.call-start = ((), (), s32[]{:S(2)}) async-start(), calls=%async_computation.4 | async-start | bytes 3145728 | tf_op jit(solution)/shard_map/psum | solution.py:116
  12.7 5.3 copy-start.9
  13.4 5.6 %copy-start.13 = (f32[2,512,3,64]{1,0,3,2:T(2,128)}, f32[2,512,3,64]{1,0,3,2:T(2,128)S(1)}, u32[]{:S(2)}) copy-start(f32[2,512,3,64]{1,0,3,2:T(2,128)S(1)} %squeeze.7) | copy-start | bytes 2359300
  15.5 3.5 copy-start.40
  18.0 2.6 copy-start.2
  18.1 2.7 copy-start.26
  22.0 3.7 copy-start.59
  22.0 3.7 copy-start.60
  22.1 5.0 copy-start.56
  22.1 48.8 %copy-start.3 = (bf16[1024,768]{1,0:T(8,128)(2,1)S(1)}, bf16[1024,768]{1,0:T(8,128)(2,1)}, u32[]{:S(2)}) copy-start(bf16[1024,768]{1,0:T(8,128)(2,1)} %param.15) | copy-start | bytes 4718596
  25.2 106.1 %all-reduce.16.cloned.1.call-start = ((), (), s32[]{:S(2)}) async-start(), calls=%async_computation.5 | async-start | bytes 3145728 | tf_op jit(solution)/shard_map/psum | solution.py:128
  25.8 105.6 %copy-start.20 = (f32[768]{0:T(1024)}, f32[768]{0:T(1024)S(1)}, u32[]{:S(2)}) copy-start(f32[768]{0:T(1024)S(1)} %convert_element_type.128) | copy-start | bytes 9220
  25.8 105.5 %copy-start.27 = (f32[768]{0:T(1024)}, f32[768]{0:T(1024)S(1)}, u32[]{:S(2)}) copy-start(f32[768]{0:T(1024)S(1)} %convert_element_type.129) | copy-start | bytes 9220
  70.9 3.6 copy-start.47
  70.9 3.6 copy-start.57
  73.0 58.3 %copy-start.23 = (f32[1024]{0:T(1024)}, f32[1024]{0:T(1024)S(1)}, u32[]{:S(2)}) copy-start(f32[1024]{0:T(1024)S(1)} %broadcast_multiply_fusion.1) | copy-start | bytes 12292
  74.6 56.8 %copy-start.30 = (f32[1024]{0:T(1024)}, f32[1024]{0:T(1024)S(1)}, u32[]{:S(2)}) copy-start(f32[1024]{0:T(1024)S(1)} %fusion.49) | copy-start | bytes 12292
  74.6 11.1 %copy-start.62 = (bf16[768,768]{1,0:T(8,128)(2,1)S(1)}, bf16[768,768]{1,0:T(8,128)(2,1)}, u32[]{:S(2)}) copy-start(bf16[768,768]{1,0:T(8,128)(2,1)} %param.25) | copy-start | bytes 3538948
  88.3 102.6 %all-reduce.18.cloned.1.call-start = ((), (), s32[]{:S(2)}) async-start(), calls=%async_computation.6 | async-start | bytes 3145728 | tf_op jit(solution)/shard_map/psum | solution.py:147
  131.3 3.3 copy-start.8
  131.3 3.3 copy-start.34
  136.4 3.6 copy-start.58
  136.4 3.6 copy-start.63
  136.5 3.6 copy-start.66
  136.5 4.3 copy-start.67
  140.1 4.0 copy-start.7
  140.1 4.0 copy-start.49
  147.8 145.4 %all-reduce.20.cloned.1.call-start = ((), (), s32[]{:S(2)}) async-start(), calls=%async_computation.7 | async-start | bytes 3145728 | tf_op jit(solution)/shard_map/psum | solution.py:181
  148.6 46.8 %copy-start.39 = (f32[1024]{0:T(1024)S(1)}, f32[1024]{0:T(1024)}, u32[]{:S(2)}) copy-start(f32[1024]{0:T(1024)} %copy-done.38) | copy-start | bytes 12292
  148.6 46.8 %copy-start.21 = (f32[768]{0:T(1024)S(1)}, f32[768]{0:T(1024)}, u32[]{:S(2)}) copy-start(f32[768]{0:T(1024)} %copy-done.20) | copy-start | bytes 9220
  148.6 46.8 %copy-start.24 = (f32[1024]{0:T(1024)S(1)}, f32[1024]{0:T(1024)}, u32[]{:S(2)}) copy-start(f32[1024]{0:T(1024)} %copy-done.23) | copy-start | bytes 12292
  148.6 46.8 %copy-start.28 = (f32[768]{0:T(1024)S(1)}, f32[768]{0:T(1024)}, u32[]{:S(2)}) copy-start(f32[768]{0:T(1024)} %copy-done.27) | copy-start | bytes 9220
  148.7 46.8 %copy-start.31 = (f32[1024]{0:T(1024)S(1)}, f32[1024]{0:T(1024)}, u32[]{:S(2)}) copy-start(f32[1024]{0:T(1024)} %copy-done.30) | copy-start | bytes 12292
  190.9 4.5 copy-start.5
  198.1 3.8 copy-start.19
  202.9 5.4 copy-start.14
  202.9 5.4 copy-start.41
  202.9 9.9 %slice-start = ((s8[6291456]{0:T(1024)(128)(4,1)}), s8[4194304]{0:T(1024)(128)(4,1)S(1)}, s32[]{:S(2)}) async-start(s8[6291456]{0:T(1024)(128)(4,1)} %bitcast.84), calls=%async_computation.12 | async-start | bytes 8388608
  208.3 4.6 slice-start.1
  219.8 3.9 copy-start.12
  223.6 108.8 %reduce-scatter.17.cloned.1.call-start = ((), (), s32[]{:S(2)}) async-start(), calls=%async_computation.11 | async-start | bytes 884736
  227.5 2.9 copy-start.17
  230.3 171.6 %reduce-scatter.15.cloned.1.call-start = ((), (), s32[]{:S(2)}) async-start(), calls=%async_computation.10 | async-start | bytes 2211840
  232.7 3.1 copy-start.50
  235.8 5.6 %copy-start.22 = (f32[768]{0:T(1024)S(1)}, f32[768]{0:T(1024)}, u32[]{:S(2)}) copy-start(f32[768]{0:T(1024)} %copy-done.20) | copy-start | bytes 9220
  235.8 5.6 %copy-start.25 = (f32[1024]{0:T(1024)S(1)}, f32[1024]{0:T(1024)}, u32[]{:S(2)}) copy-start(f32[1024]{0:T(1024)} %copy-done.23) | copy-start | bytes 12292
  235.8 5.6 %copy-start.29 = (f32[768]{0:T(1024)S(1)}, f32[768]{0:T(1024)}, u32[]{:S(2)}) copy-start(f32[768]{0:T(1024)} %copy-done.27) | copy-start | bytes 9220
  235.8 5.6 %copy-start.32 = (f32[1024]{0:T(1024)S(1)}, f32[1024]{0:T(1024)}, u32[]{:S(2)}) copy-start(f32[1024]{0:T(1024)} %copy-done.30) | copy-start | bytes 12292
  235.8 5.6 %copy-start.48 = (f32[768]{0:T(1024)S(1)}, f32[768]{0:T(1024)}, u32[]{:S(2)}) copy-start(f32[768]{0:T(1024)} %convert_element_type.130) | copy-start | bytes 9220
  235.8 238.3 %reduce-scatter.13.cloned.1.call-start = ((), (), s32[]{:S(2)}) async-start(), calls=%async_computation.9 | async-start | bytes 2654208 | tf_op jit(solution)/shard_map/reduce_scatter | solution.py:207
  241.3 5.5 copy-start.64
  241.3 7.3 %copy-start.61 = (bf16[768]{0:T(1024)(128)(2,1)S(1)}, bf16[768]{0:T(1024)(128)(2,1)}, u32[]{:S(2)}) copy-start(bf16[768]{0:T(1024)(128)(2,1)} %param.28) | copy-start | bytes 4612
  241.3 7.3 %copy-start.55 = (f32[768]{0:T(1024)S(1)}, f32[768]{0:T(1024)}, u32[]{:S(2)}) copy-start(f32[768]{0:T(1024)} %get-tuple-element.86) | copy-start | bytes 9220
  241.3 7.4 %copy-start.35 = (f32[768]{0:T(1024)S(1)}, f32[768]{0:T(1024)}, u32[]{:S(2)}) copy-start(f32[768]{0:T(1024)} %convert_element_type.136) | copy-start | bytes 9220
  241.3 305.1 %reduce-scatter.11.cloned.1.call-start = ((), (), s32[]{:S(2)}) async-start(), calls=%async_computation.8 | async-start | bytes 2654208 | tf_op jit(solution)/shard_map/reduce_scatter | solution.py:205
  246.7 4.0 copy-start.53
  246.7 4.0 copy-start.42
  246.7 4.0 copy-start.44
  246.7 4.1 copy-start.45
  246.7 4.1 copy-start.46
  246.7 4.1 copy-start.51
  246.7 4.1 copy-start.52
  246.7 299.7 %copy-start.1 = (bf16[768,768]{1,0:T(8,128)(2,1)S(1)}, bf16[768,768]{1,0:T(8,128)(2,1)}, u32[]{:S(2)}) copy-start(bf16[768,768]{1,0:T(8,128)(2,1)} %param.23) | copy-start | bytes 3538948
  (15 other events, 22.5 us)
Sparse Core Ops, SparseCore 0:
  25.3 45.5 all-reduce.13
  88.4 42.8 all-reduce.15
  147.9 42.8 all-reduce.17
  223.7 42.9 all-reduce.19
  269.8 62.5 reduce-scatter.16
  336.2 65.7 reduce-scatter.14
  406.0 68.0 reduce-scatter.12
  478.2 68.1 reduce-scatter.10
where the time goes:
time: 560 us; the launch traced here: 553 us
  waiting for transfers between devices  374 us (67%)
  matrix products  58.2 us (10%)
  blocking collectives  37.6 us (7%)
  other arithmetic  33.5 us (6%)
  local copies, waits for them, and re-layouts  33.2 us (6%)
  between operations  16.7 us (3%)
    unnamed x10, waiting for transfers between devices  105 us
    reduce_scatter x1, waiting for transfers between devices, body(): lax.psum_scatter(up_grad, 'dp', scatter_dimension=0, tiled=True)  72.3 us
    reduce_scatter x1, waiting for transfers between devices, body(): lax.psum_scatter(down_grad, 'dp', scatter_dimension=1, tiled=True)  70.4 us
    psum x1, waiting for transfers between devices, body(): lax.psum(attn_terms.astype(jnp.bfloat16), 'tensor').astype(jnp.float32)  43.2 us
    psum x1, waiting for transfers between devices, body(): lax.psum(up_terms.astype(jnp.bfloat16), 'tensor').astype(jnp.float32)  42.2 us
    psum x1, waiting for transfers between devices, body(): lax.psum(down_terms.astype(jnp.bfloat16), 'tensor').astype(jnp.float32)  40.5 us
    unnamed x1, blocking collectives  37.6 us
    unnamed x161, local copies, waits for them, and re-layouts  25.7 us
  transfers between devices with their start and end apart: 8, of which 7 were waited for; matrix products, arithmetic and copies ran while one was open for 7% of the time, Pallas kernels for 0%

commit v1 on v0

--- a/solution.py
+++ b/solution.py
@@ -144,7 +144,9 @@
     d_hidden_low = d_hidden.astype(jnp.bfloat16)
     up_grad = jnp.einsum("td,tf->df", first_low, d_hidden_low, preferred_element_type=jnp.float32)
     up_terms = jnp.einsum("tf,df->td", d_hidden_low, up_weight, preferred_element_type=jnp.float32)
-    up_total = lax.psum(up_terms.astype(jnp.bfloat16), "tensor").astype(jnp.float32)
+    up_total = jnp.sum(lax.all_gather(up_terms.astype(jnp.bfloat16), "tensor"), axis=0).astype(
+        jnp.float32
+    )
     d_first = d_second + up_total
     d_first_in, gain_first_grad, shift_first_grad = norm_back(
         first_in, gain_first, shift_first, d_first

time: 560 us -> 569 us (1.016)
    all_gather x0 -> x1, waiting for transfers between devices: none -> 45.8 us  [body(): lax.all_gather(up_terms.astype(jnp.bfloat16), 'tensor')]
    psum x1 -> x0, waiting for transfers between devices: 42.2 us -> none  [body(): lax.psum(up_terms.astype(jnp.bfloat16), 'tensor').astype(jnp.float32)]
    unnamed x161 -> x163, local copies, waits for them, and re-layouts: 25.7 us -> 25.6 us
where the time goes in v1:
time: 569 us; the launch traced here: 562 us
  waiting for transfers between devices  377 us (66%)
  matrix products  58.3 us (10%)
  other arithmetic  39 us (7%)
  blocking collectives  37.5 us (7%)
  local copies, waits for them, and re-layouts  33.2 us (6%)
  between operations  16.6 us (3%)
    unnamed x10, waiting for transfers between devices  105 us
    reduce_scatter x1, waiting for transfers between devices, body(): lax.psum_scatter(up_grad, 'dp', scatter_dimension=0, tiled=True)  72.1 us
    reduce_scatter x1, waiting for transfers between devices, body(): lax.psum_scatter(down_grad, 'dp', scatter_dimension=1, tiled=True)  70.4 us
    all_gather x1, waiting for transfers between devices, body(): lax.all_gather(up_terms.astype(jnp.bfloat16), 'tensor')  45.8 us
    psum x1, waiting for transfers between devices, body(): lax.psum(attn_terms.astype(jnp.bfloat16), 'tensor').astype(jnp.float32)  43.2 us
    psum x1, waiting for transfers between devices, body(): lax.psum(down_terms.astype(jnp.bfloat16), 'tensor').astype(jnp.float32)  40.5 us
    unnamed x1, blocking collectives  37.5 us
    unnamed x163, local copies, waits for them, and re-layouts  25.6 us
  transfers between devices with their start and end apart: 8, of which 7 were waited for; matrix products, arithmetic and copies ran while one was open for 7% of the time, Pallas kernels for 0%

profile of v1, /device:TPU:0, one launch (start us, length us, event | category | flops | bytes accessed | tf_op | source)
XLA Modules:
  0.0 562.4 jit_solution(16559771452155627336)
XLA Ops:
  7.2 2.8 fusion.21
  10.2 1.0 fusion.64
  11.2 1.2 broadcast_compare_fusion
  12.7 0.7 squeeze.7
  13.4 2.1 squeeze.8
  15.5 2.5 fusion.66
  18.0 0.9 fusion
  19.0 1.7 copy-done.2
  20.7 1.3 fusion.29
  22.5 0.8 copy-done.11
  23.3 1.8 convolution_convert_fusion.3
  25.7 1.3 convert_element_type.132
  27.0 0.7 reshape.183
  27.6 43.2 %all-reduce.13.cloned.1.call-done = bf16[1024,768]{1,0:T(8,128)(2,1)} async-done(((bf16[1024,768]{1,0:T(8,128)(2,1)}), bf16[1024,768]{1,0:T(8,128)(2,1)}) %all-reduce.13.cloned.1.call-update) | async-done | bytes 1572880 | tf_op jit(solution)/shard_map/psum | solution.py:116
  70.8 2.1 fusion.17
  73.0 0.9 multiply_reduce_fusion.4
  73.9 0.6 copy-done.38
  74.5 9.9 %multiply_convert_fusion.1 = (bf16[1024,768]{1,0:T(8,128)(2,1)S(1)}, f32[1024,768]{1,0:T(8,128)}, f32[1024,768]{1,0:T(8,128)}) fusion(f32[768]{0:T(1024)S(1)} %copy-done.58, bf16[768,768]{1,0:T(8,128)(2,1)S(1)} %copy-done, f32[768]{0:T(1024)S(1)} %copy-done.47, f32[768]{0:T(1024)S(1)} %convert_element_type.131, f32[1024]{0:T(1024)S(1)} %fusion.49, ...), kind=kOutput, calls=%fused_computation.27 | convolution fusion | flops 1266941952 | bytes 12210176 | tf_op jit(solution)/shard_map/dot_general | solution.py:122
  84.4 1.2 copy-done.66
  85.5 2.6 convolution_convert_fusion.2
  88.2 1.3 convert_element_type.138
  89.5 1.3 convert_element_type.137
  90.7 40.5 %all-reduce.15.cloned.1.call-done = bf16[1024,768]{1,0:T(8,128)(2,1)} async-done(((bf16[1024,768]{1,0:T(8,128)(2,1)}), bf16[1024,768]{1,0:T(8,128)(2,1)}) %all-reduce.15.cloned.1.call-update) | async-done | bytes 1572880 | tf_op jit(solution)/shard_map/psum | solution.py:128
  131.2 3.3 fusion.62
  134.5 1.8 fusion.4
  136.4 3.6 fusion.61
  140.0 0.7 copy-done.68
  140.7 3.2 fusion.69
  143.9 1.2 copy-done.69
  145.1 2.7 convolution_convert_fusion.1
  147.9 0.7 log_add_fusion
  148.6 45.8 %all-gather.3.cloned.1.call-done = bf16[4096,768]{1,0:T(8,128)(2,1)} async-done(((bf16[1024,768]{1,0:T(8,128)(2,1)}), bf16[4096,768]{1,0:T(8,128)(2,1)}) %all-gather.3.cloned.1.call-update) | async-done | bytes 6291472 | tf_op jit(solution)/shard_map/all_gather | solution.py:147
  194.4 5.4 reduce_sum.191
  199.8 4.6 fusion.59
  204.4 2.7 multiply_reduce_fusion.1
  207.1 2.1 fusion.60
  209.2 1.7 copy-done.6
  210.9 0.7 convolution_convert_fusion.4
  211.9 5.4 fusion.67
  217.3 4.5 multiply_reduce_fusion
  221.9 1.8 multiply_convert_fusion
  223.7 1.1 fusion.26
  224.8 0.7 fusion.68
  227.8 1.0 copy-done.16
  228.8 3.9 convolution_convert_fusion
  232.7 2.4 fusion.19
  235.1 1.5 copy.79
  236.6 2.8 reshape.191
  239.5 2.3 convolution_bitcast_fusion
  241.8 3.0 copy.83
  244.9 5.4 fusion.51
  250.5 5.2 fusion.37
  255.8 0.6 dynamic-slice
  257.8 2.0 fusion.32
  259.8 37.5 %all-reduce.8 = (f32[2,3,64]{2,1,0:T(4,128)S(1)}, f32[768]{0:T(1024)S(1)}, f32[768]{0:T(1024)S(1)}, f32[768]{0:T(1024)S(1)}, f32[12,64]{1,0:T(8,128)S(1)}, /*ind...) all-reduce(f32[2,3,64]{2,1,0:T(4,128)S(1)} %pad_maximum_fusion, ...), channel_id=4, replica_groups=mesh['dp'=8,'tensor'=4] {'dp'}, use_global_device_ids=true, to_apply=%region_18.19.clone | all-reduce | flops 5760 | bytes 46080
  298.0 0.7 copy.70
  302.2 2.1 fusion.30
  304.2 37.2 %reduce-scatter.17.cloned.1.call-done = f32[96,192]{1,0:T(8,128)} async-done(((f32[768,192]{1,0:T(8,128)}), f32[96,192]{1,0:T(8,128)}) %reduce-scatter.17.cloned.1.call-update) | async-done | bytes 73744
  341.4 1.0 reshape.192
  342.5 0.8 copy.80
  343.2 67.7 %reduce-scatter.15.cloned.1.call-done = f32[96,576]{1,0:T(8,128)} async-done(((f32[768,576]{1,0:T(8,128)}), f32[96,576]{1,0:T(8,128)}) %reduce-scatter.15.cloned.1.call-update) | async-done | bytes 221200
  410.9 1.8 copy.84
  412.7 70.4 %reduce-scatter.13.cloned.1.call-done = f32[768,96]{0,1:T(8,128)} async-done(((f32[768,768]{0,1:T(8,128)}), f32[768,96]{0,1:T(8,128)}) %reduce-scatter.13.cloned.1.call-update) | async-done | bytes 294928 | tf_op jit(solution)/shard_map/reduce_scatter | solution.py:209
  483.2 72.1 %reduce-scatter.11.cloned.1.call-done = f32[96,768]{1,0:T(8,128)} async-done(((f32[768,768]{1,0:T(8,128)}), f32[96,768]{1,0:T(8,128)}) %reduce-scatter.11.cloned.1.call-update) | async-done | bytes 294928 | tf_op jit(solution)/shard_map/reduce_scatter | solution.py:207
  (189 shorter events, 8.9 us)
Async XLA Ops:
  7.2 67.3 %copy-start = (bf16[768,768]{1,0:T(8,128)(2,1)S(1)}, bf16[768,768]{1,0:T(8,128)(2,1)}, u32[]{:S(2)}) copy-start(bf16[768,768]{1,0:T(8,128)(2,1)} %param.23) | copy-start | bytes 3538948
  7.2 63.6 %all-reduce.13.cloned.1.call-start = ((), (), s32[]{:S(2)}) async-start(), calls=%async_computation.4 | async-start | bytes 3145728 | tf_op jit(solution)/shard_map/psum | solution.py:116
  12.7 5.3 copy-start.9
  13.4 5.6 copy-start.13
  15.5 3.5 copy-start.40
  18.0 2.7 copy-start.26
  22.0 3.6 copy-start.60
  22.0 3.6 copy-start.61
  22.0 4.9 copy-start.57
  22.0 48.8 %copy-start.3 = (bf16[1024,768]{1,0:T(8,128)(2,1)S(1)}, bf16[1024,768]{1,0:T(8,128)(2,1)}, u32[]{:S(2)}) copy-start(bf16[1024,768]{1,0:T(8,128)(2,1)} %param.15) | copy-start | bytes 4718596
  25.1 106.1 %all-reduce.15.cloned.1.call-start = ((), (), s32[]{:S(2)}) async-start(), calls=%async_computation.5 | async-start | bytes 3145728 | tf_op jit(solution)/shard_map/psum | solution.py:128
  25.7 105.5 %copy-start.20 = (f32[768]{0:T(1024)}, f32[768]{0:T(1024)S(1)}, u32[]{:S(2)}) copy-start(f32[768]{0:T(1024)S(1)} %convert_element_type.130) | copy-start | bytes 9220
  25.7 105.5 %copy-start.27 = (f32[768]{0:T(1024)}, f32[768]{0:T(1024)S(1)}, u32[]{:S(2)}) copy-start(f32[768]{0:T(1024)S(1)} %convert_element_type.131) | copy-start | bytes 9220
  70.8 3.6 copy-start.47
  70.8 3.6 copy-start.58
  72.9 58.2 %copy-start.23 = (f32[1024]{0:T(1024)}, f32[1024]{0:T(1024)S(1)}, u32[]{:S(2)}) copy-start(f32[1024]{0:T(1024)S(1)} %broadcast_multiply_fusion.1) | copy-start | bytes 12292
  74.5 56.7 %copy-start.30 = (f32[1024]{0:T(1024)}, f32[1024]{0:T(1024)S(1)}, u32[]{:S(2)}) copy-start(f32[1024]{0:T(1024)S(1)} %fusion.49) | copy-start | bytes 12292
  74.5 11.1 %copy-start.63 = (bf16[768,768]{1,0:T(8,128)(2,1)S(1)}, bf16[768,768]{1,0:T(8,128)(2,1)}, u32[]{:S(2)}) copy-start(bf16[768,768]{1,0:T(8,128)(2,1)} %param.25) | copy-start | bytes 3538948
  88.1 106.3 %all-gather.3.cloned.1.call-start = ((), (), s32[]{:S(2)}) async-start(), calls=%async_computation.9 | async-start | bytes 7864320 | tf_op jit(solution)/shard_map/all_gather | solution.py:147
  131.2 3.3 copy-start.8
  131.2 3.3 copy-start.34
  136.3 3.6 copy-start.59
  136.3 3.6 copy-start.64
  136.3 3.6 copy-start.67
  136.3 4.3 copy-start.68
  139.9 4.0 copy-start.7
  139.9 4.0 copy-start.49
  147.8 154.4 %all-reduce.17.cloned.1.call-start = ((), (), s32[]{:S(2)}) async-start(), calls=%async_computation.6 | async-start | bytes 3145728 | tf_op jit(solution)/shard_map/psum | solution.py:183
  194.4 5.4 copy-start.21
  194.4 5.4 copy-start.24
  194.4 5.4 copy-start.28
  194.4 5.4 copy-start.50
  199.8 4.6 copy-start.39
  199.8 4.6 copy-start.5
  199.8 4.6 copy-start.31
  207.1 3.8 copy-start.19
  211.9 5.4 copy-start.14
  211.9 5.4 copy-start.41
  211.9 9.9 %slice-start = ((s8[6291456]{0:T(1024)(128)(4,1)}), s8[4194304]{0:T(1024)(128)(4,1)S(1)}, s32[]{:S(2)}) async-start(s8[6291456]{0:T(1024)(128)(4,1)} %bitcast.85), calls=%async_computation.12 | async-start | bytes 8388608
  217.3 4.6 slice-start.1
  228.8 3.9 copy-start.12
  232.6 108.8 %reduce-scatter.17.cloned.1.call-start = ((), (), s32[]{:S(2)}) async-start(), calls=%async_computation.11 | async-start | bytes 884736
  236.6 2.9 copy-start.17
  239.4 171.5 %reduce-scatter.15.cloned.1.call-start = ((), (), s32[]{:S(2)}) async-start(), calls=%async_computation.10 | async-start | bytes 2211840
  241.8 3.1 copy-start.51
  244.8 5.6 copy-start.22
  244.8 5.6 copy-start.25
  244.8 5.6 copy-start.29
  244.9 5.6 copy-start.32
  244.9 5.6 copy-start.48
  244.9 238.3 %reduce-scatter.13.cloned.1.call-start = ((), (), s32[]{:S(2)}) async-start(), calls=%async_computation.8 | async-start | bytes 2654208 | tf_op jit(solution)/shard_map/reduce_scatter | solution.py:209
  250.3 5.5 copy-start.65
  250.3 7.4 %copy-start.62 = (bf16[768]{0:T(1024)(128)(2,1)S(1)}, bf16[768]{0:T(1024)(128)(2,1)}, u32[]{:S(2)}) copy-start(bf16[768]{0:T(1024)(128)(2,1)} %param.28) | copy-start | bytes 4612
  250.4 7.4 %copy-start.56 = (f32[768]{0:T(1024)S(1)}, f32[768]{0:T(1024)}, u32[]{:S(2)}) copy-start(f32[768]{0:T(1024)} %get-tuple-element.86) | copy-start | bytes 9220
  250.4 7.4 %copy-start.35 = (f32[768]{0:T(1024)S(1)}, f32[768]{0:T(1024)}, u32[]{:S(2)}) copy-start(f32[768]{0:T(1024)} %convert_element_type.138) | copy-start | bytes 9220
  250.4 304.9 %reduce-scatter.11.cloned.1.call-start = ((), (), s32[]{:S(2)}) async-start(), calls=%async_computation.7 | async-start | bytes 2654208 | tf_op jit(solution)/shard_map/reduce_scatter | solution.py:207
  255.7 4.0 copy-start.54
  255.7 4.0 copy-start.42
  255.7 4.1 copy-start.44
  255.7 4.1 copy-start.45
  255.7 4.1 copy-start.46
  255.7 4.1 copy-start.52
  255.7 4.1 copy-start.53
  255.8 299.5 %copy-start.1 = (bf16[768,768]{1,0:T(8,128)(2,1)S(1)}, bf16[768,768]{1,0:T(8,128)(2,1)}, u32[]{:S(2)}) copy-start(bf16[768,768]{1,0:T(8,128)(2,1)} %param.23) | copy-start | bytes 3538948
  (16 other events, 25.2 us)
Sparse Core Ops, SparseCore 0:
  25.2 45.5 all-reduce.12
  88.2 42.8 all-reduce.14
  147.9 46.4 all-gather.2
  232.8 42.8 all-reduce.16
  278.8 62.5 reduce-scatter.16
  345.2 65.6 reduce-scatter.14
  415.0 68.1 reduce-scatter.12
  487.2 68.0 reduce-scatter.10
